TPU v7x, 256 devices: a whole 4x4x8 slice. The times are simulated.
256 devices in a mesh: side: 2 (over y_hi), row: 8 (over z), col: 16 (over x, y_lo, core).
Axes of the slice: x: 4, y: 4 (y_hi: 2, y_lo: 2; y = y_hi * 2 + y_lo), z: 8, core: 2. Of those that a mesh axis runs over, the one named last changes fastest.
Arguments:
- queries: bfloat16 [512, 8192], P(('row', 'col')), may hold values from -4.5 to 16
- new_entries: bfloat16 [512, 2048], P(('row', 'col')), may hold values from -4.5 to 15.875
- cache_keys: bfloat16 [2, 512, 256, 1024], P('side', ('row', 'col')), may hold values from -4.5 to 16
- cache_values: bfloat16 [2, 512, 256, 1024], P('side', ('row', 'col')), may hold values from -6 to 6
- lengths: int32 [512], P(('row', 'col')), may hold values from 1 to 256, 32768 in all
- residual: bfloat16 [512, 8192], P(None, 'col'), may hold values from -16 to 16
- norm_gain: bfloat16 [8192], P('col'), may hold values from 0.099609375 to 1.8984375
- out_weight: bfloat16 [2, 8192, 8192], P('side', 'row', 'col'), may hold values from -0.125 to 0.125
- gate_weight: bfloat16 [2, 8192, 14336], P('side', 'col', 'row'), may hold values from -0.0625 to 0.0625
- up_weight: bfloat16 [2, 8192, 14336], P('side', 'col', 'row'), may hold values from -0.0625 to 0.0625
- down_weight: bfloat16 [2, 14336, 8192], P('side', 'row', 'col'), may hold values from -0.046875 to 0.046875
Outputs:
- layer_out: bfloat16 [512, 8192], P(('row', 'col'), 'side')
All inputs are finite; a program needn't handle non-finite values. No bound on the sum of `lengths` on one device may be relied on, other than what follows from the above.
Results may differ from a plain program's by a relative error of at most 0.025.
Values may be sent and summed in bfloat16 or wider, within the bound.
No kernel may reach another device: no remote copies, remote signals or barrier semaphores. Data moves between devices by JAX's collectives and lax.ppermute only.
A program may use at most 64 MiB of HBM per device.

v0:
```python
import jax
import jax.numpy as jnp
from jax import lax
from jax.sharding import PartitionSpec as P

D = 8192
H = 64
KVH = 8
HD = 128
ORIG = 64
rope_theta = 500000.0
stretch_factor = 8.0
eps = 1e-05


def from_behind(value, axis, steps):
    count = lax.axis_size(axis)
    first, last = (max(0, -steps), min(count, count - steps))
    return lax.ppermute(value, axis, [(source, source + steps) for source in range(first, last)])


def frequencies(lengths):
    seq = lengths.astype(jnp.float32) + 1.0
    stretch = jnp.maximum(stretch_factor * seq / ORIG - (stretch_factor - 1.0), 1.0)
    log_base = jnp.log(jnp.float32(rope_theta)) + HD / (HD - 2.0) * jnp.log(stretch)
    expo = jnp.arange(HD // 2).astype(jnp.float32) * (2.0 / HD)
    return jnp.exp(-expo[None, :] * log_base[:, None])


def rotary(vec, angles):
    half = vec.shape[-1] // 2
    first = vec[..., :half]
    second = vec[..., half:]
    cosine = jnp.cos(angles)
    sine = jnp.sin(angles)
    return jnp.concatenate(
        [first * cosine - second * sine, second * cosine + first * sine], axis=-1
    )


def attention(queries, new_entries, keys, values, lengths):
    slots = queries.shape[0]
    span = keys.shape[1]
    per_group = H // KVH
    freqs = frequencies(lengths)
    angle_new = lengths.astype(jnp.float32)[:, None] * freqs
    angle_cache = jnp.arange(span).astype(jnp.float32)[None, :, None] * freqs[:, None, :]
    query_rot = rotary(
        queries.astype(jnp.float32).reshape(slots, H, HD), angle_new[:, None, :]
    ).astype(jnp.bfloat16)
    query_rot = query_rot.reshape(slots, KVH, per_group, HD)
    key_fresh = new_entries[:, : KVH * HD].astype(jnp.float32).reshape(slots, KVH, HD)
    value_fresh = new_entries[:, KVH * HD :].astype(jnp.float32).reshape(slots, KVH, HD)
    key_new_rot = rotary(key_fresh, angle_new[:, None, :]).astype(jnp.bfloat16)
    key_rot = rotary(
        keys.astype(jnp.float32).reshape(slots, span, KVH, HD), angle_cache[:, :, None, :]
    ).astype(jnp.bfloat16)
    scale = HD ** (-0.5)
    scores = (
        jnp.einsum("sgqd,scgd->sgqc", query_rot, key_rot, preferred_element_type=jnp.float32)
        * scale
    )
    own_score = (
        jnp.einsum("sgqd,sgd->sgq", query_rot, key_new_rot, preferred_element_type=jnp.float32)
        * scale
    )
    valid_mask = (jnp.arange(span)[None, :] < lengths[:, None])[:, None, None, :]
    highest = jnp.maximum(jnp.max(jnp.where(valid_mask, scores, -1e30), axis=-1), own_score)
    weights = jnp.where(valid_mask, jnp.exp(scores - highest[..., None]), 0.0)
    own_weight = jnp.exp(own_score - highest)
    totals = jnp.sum(weights, axis=-1) + own_weight
    weights16 = weights.astype(jnp.bfloat16)
    mixed = jnp.einsum(
        "sgqc,scgd->sgqd",
        weights16,
        values.reshape(slots, span, KVH, HD),
        preferred_element_type=jnp.float32,
    )
    mixed = mixed + own_weight[..., None] * value_fresh[:, :, None, :]
    return (mixed / totals[..., None]).reshape(slots, H * HD).astype(jnp.bfloat16)


def local(
    queries,
    new_entries,
    cache_keys,
    cache_values,
    lengths,
    residual,
    norm_gain,
    out_weight,
    gate_weight,
    up_weight,
    down_weight,
):
    attended = attention(queries, new_entries, cache_keys[0], cache_values[0], lengths)
    slot_count = attended.shape[0]
    row_count = lax.axis_size("row")
    col_count = lax.axis_size("col")
    head_block = attended.shape[1] // row_count
    split_heads = attended.reshape(slot_count, row_count, head_block)
    moved = from_behind(split_heads, "side", 1)
    blocks = lax.all_to_all(moved, "row", split_axis=1, concat_axis=0, tiled=True)
    sectioned = blocks.reshape(row_count, 1, slot_count, head_block)
    out_block = out_weight[0]
    partial_value = jnp.einsum(
        "akjd,de->akje",
        lax.all_gather(sectioned, "col", axis=1, tiled=True),
        out_block,
        preferred_element_type=jnp.float32,
    )
    col_width = out_block.shape[1]
    total_rows = row_count * col_count * slot_count
    projected = lax.psum(
        partial_value.reshape(total_rows, col_width).astype(jnp.bfloat16), "row"
    ).astype(jnp.float32)
    stream = residual.astype(jnp.float32) + projected
    squares = lax.psum(jnp.sum(stream * stream, axis=1), "col")
    inv_rms = lax.rsqrt(squares / D + eps)
    normed = (stream * inv_rms[:, None] * norm_gain.astype(jnp.float32)[None, :]).astype(
        jnp.bfloat16
    )
    gate_block = gate_weight[0]
    up_block = up_weight[0]
    down_block = down_weight[0]
    gate_part = jnp.dot(normed, gate_block, preferred_element_type=jnp.float32)
    up_part = jnp.dot(normed, up_block, preferred_element_type=jnp.float32)
    gate_total, up_total = (
        lax.psum(gate_part.astype(jnp.bfloat16), "col").astype(jnp.float32),
        lax.psum(up_part.astype(jnp.bfloat16), "col").astype(jnp.float32),
    )
    hidden = (jax.nn.silu(gate_total) * up_total).astype(jnp.bfloat16)
    down_part = jnp.dot(hidden, down_block, preferred_element_type=jnp.float32)
    down_total = lax.psum(down_part.astype(jnp.bfloat16), "row").astype(jnp.float32)
    final = (stream + down_total).astype(jnp.bfloat16)
    group_rows = col_count * slot_count
    mine_rows = lax.dynamic_slice_in_dim(final, lax.axis_index("row") * group_rows, group_rows, 0)
    slot_rows = lax.all_to_all(mine_rows, "col", split_axis=0, concat_axis=1, tiled=True)
    half_width = slot_rows.shape[1] // 2
    returned = from_behind(slot_rows[:, :half_width], "side", -1)
    return jnp.where(lax.axis_index("side") == 0, returned, slot_rows[:, half_width:])


def solution(mesh):
    in_specs = (
        P(("row", "col"), None),
        P(("row", "col"), None),
        P("side", ("row", "col"), None, None),
        P("side", ("row", "col"), None, None),
        P(("row", "col")),
        P(None, "col"),
        P("col"),
        P("side", "row", "col"),
        P("side", "col", "row"),
        P("side", "col", "row"),
        P("side", "row", "col"),
    )
    out_specs = P(("row", "col"), "side")
    return jax.shard_map(local, mesh=mesh, in_specs=in_specs, out_specs=out_specs, check_vma=False)
```

profile of v0, /device:TPU:1, one launch (start us, length us, event | category | flops | bytes accessed | tf_op | source)
XLA Modules:
  0.0 439.4 jit_solution(3323142169381161737)
XLA Ops:
  6.5 0.8 convert_element_type.82
  7.3 0.7 multiply_add_fusion
  8.0 0.7 iota_compare_fusion
  8.7 3.9 copy.23
  12.7 4.2 fusion.50
  16.8 3.8 copy.32
  20.6 3.8 copy.33
  24.9 1.9 multiply_cosine_fusion
  27.1 4.7 %subtract_convert_fusion = (bf16[4,256,8,64]{3,1,2,0:T(8,128)(2,1)S(1)}, bf16[4,256,8,64]{3,1,2,0:T(8,128)(2,1)S(1)}) fusion(f32[4,256,8,64]{3,1,2,0:T(8,128)} %copy.33, f32[4,256,8,64]{3,1,2,0:T(8,128)} %copy.32, f32[4,256,64]{2,1,0:T(8,128)S(1)} %get-tuple-element.22, f32[4,256,64]{2,1,0:T(8,128)S(1)} %get-tuple-element.21), kind=kLoop, calls=%fused_computation.3 | loop fusion | flops 4194304 | bytes 6815744 | tf_op jit(solution)/shard_map/convert.6
  31.8 1.3 select_reduce_fusion
  33.4 0.6 copy.36
  34.0 0.4 fusion.30
  34.6 5.7 %collective-permute-start = (bf16[4,8,1024]{2,0,1:T(4,128)(2,1)S(1)}, bf16[4,8,1024]{2,0,1:T(4,128)(2,1)S(1)}, u32[]{:S(2)}, u32[]{:S(2)}) collective-permute-start(bf16[4,8,1024]{2,0,1:T(4,128)(2,1)S(1)} %copy.27), channel_id=1, source_target_pairs={{0,128},{1,129},{2,130},{3,131},{4,132},{5,133},{6,134},{7,135},{8... | collective-permute-start | bytes 196616 | tf_op jit(solution)/shard_map/ppermute | solution.py:19
  40.3 1.3 collective-permute-done
  41.6 15.3 %all_to_all.34 = bf16[4,8,1024]{2,0,1:T(4,128)(2,1)S(1)} all-to-all(bf16[4,8,1024]{2,0,1:T(4,128)(2,1)S(1)} %collective-permute-done), channel_id=1, replica_groups=mesh['side'=2,'row'=8,'col'=16] {'row'}, dimensions={1} | all-to-all | bytes 131072 | tf_op jit(solution)/shard_map/all_to_all | solution.py:103
  56.9 0.6 copy.28
  57.6 34.6 %all-gather.3.cloned.1.call-done = bf16[8,64,1,1024]{3,0,2,1:T(8,128)(2,1)} async-done(((bf16[8,4,1,1024]{3,0,2,1:T(8,128)(2,1)}), bf16[8,64,1,1024]{3,0,2,1:T(8,128)(2,1)}) %all-gather.3.cloned.1.call-update) | async-done | bytes 1048592 | tf_op jit(solution)/shard_map/all_gather | solution.py:108
  92.2 1.8 copy.29
  94.1 2.8 convolution_convert_fusion.2
  96.9 68.6 %all-reduce.5.cloned.1.call-done = bf16[512,512]{1,0:T(8,128)(2,1)} async-done(((bf16[512,512]{1,0:T(8,128)(2,1)}), bf16[512,512]{1,0:T(8,128)(2,1)}) %all-reduce.5.cloned.1.call-update) | async-done | bytes 524304 | tf_op jit(solution)/shard_map/psum | solution.py:114
  165.5 1.3 multiply_reduce_fusion
  166.8 31.7 %psum.36 = f32[512]{0:T(512)S(1)} all-reduce(f32[512]{0:T(512)S(1)} %get-tuple-element.13), channel_id=1, replica_groups=mesh['side'=2,'row'=8,'col'=16] {'col'}, use_global_device_ids=true, to_apply=%region_4.5 | all-reduce | flops 512 | bytes 4096 | tf_op jit(solution)/shard_map/psum | solution.py:118
  198.6 3.6 convolution_convert_fusion.1
  202.2 2.5 convolution_convert_fusion
  204.8 129.6 %all-reduce.9.cloned.1.call-done = (bf16[512,1792]{1,0:T(8,128)(2,1)}, bf16[512,1792]{1,0:T(8,128)(2,1)}) async-done(((bf16[512,1792]{1,0:T(8,128)(2,1)}, bf16[512,1792]{1,0:T(8,128)(2,1)}), (bf16[512,1792]{1,0:T(8,128)(2,1)}, bf16[512,1792]{1,0:T(8,128)(2,1)})) %all-reduce.9.cloned.1.call-update) | async-done | bytes 3670032 | tf_op jit(solution)/shard_map/psum | solution.py:130
  334.4 4.6 %fusion.16 = bf16[512,512]{1,0:T(8,128)(2,1)} fusion(bf16[1,1792,512]{2,1,0:T(8,128)(2,1)} %param.21, bf16[512,1792]{1,0:T(8,128)(2,1)} %get-tuple-element.5, bf16[512,1792]{1,0:T(8,128)(2,1)} %get-tuple-element.6), kind=kOutput, calls=%fused_computation.21 | convolution fusion | flops 947126272 | bytes 6029312 | tf_op jit(solution)/shard_map/dot_general | solution.py:133
  339.0 70.0 %all-reduce.7.cloned.1.call-done = bf16[512,512]{1,0:T(8,128)(2,1)} async-done(((bf16[512,512]{1,0:T(8,128)(2,1)}), bf16[512,512]{1,0:T(8,128)(2,1)}) %all-reduce.7.cloned.1.call-update) | async-done | bytes 524304 | tf_op jit(solution)/shard_map/psum | solution.py:134
  409.1 0.9 fusion.37
  409.9 16.1 %all_to_all.35 = bf16[16,4,512]{2,1,0:T(4,128)(2,1)S(1)} all-to-all(bf16[16,4,512]{2,1,0:T(4,128)(2,1)S(1)} %all_to_all.28), channel_id=1, replica_groups=mesh['side'=2,'row'=8,'col'=16] {'col'}, dimensions={0} | all-to-all | bytes 131072 | tf_op jit(solution)/shard_map/all_to_all | solution.py:138
  426.0 1.3 collective-permute-start.1
  427.3 4.9 %collective-permute-done.1 = bf16[4,4096]{1,0:T(4,128)(2,1)S(1)} collective-permute-done((bf16[4,4096]{1,0:T(4,128)(2,1)S(1)}, bf16[4,4096]{1,0:T(4,128)(2,1)S(1)}, u32[]{:S(2)}, u32[]{:S(2)}) %collective-permute-start.1) | collective-permute-done | bytes 32800 | tf_op jit(solution)/shard_map/ppermute | solution.py:19
  432.2 0.6 slice_select_fusion
  (44 shorter events, 1.2 us)
Async XLA Ops:
  6.5 192.0 %copy-start = (bf16[1,512,1792]{2,1,0:T(8,128)(2,1)S(1)}, bf16[1,512,1792]{2,1,0:T(8,128)(2,1)}, u32[]{:S(2)}) copy-start(bf16[1,512,1792]{2,1,0:T(8,128)(2,1)} %param.19) | copy-start | bytes 5505028
  6.5 85.7 %all-gather.3.cloned.1.call-start = ((), (), s32[]{:S(2)}) async-start(), calls=%async_computation.4 | async-start | bytes 1114112 | tf_op jit(solution)/shard_map/all_gather | solution.py:108
  20.6 3.8 copy-start.4
  20.6 3.9 copy-start.5
  31.8 1.6 copy-start.1
  34.6 7.0 %collective-permute-start = (bf16[4,8,1024]{2,0,1:T(4,128)(2,1)S(1)}, bf16[4,8,1024]{2,0,1:T(4,128)(2,1)S(1)}, u32[]{:S(2)}, u32[]{:S(2)}) collective-permute-start(bf16[4,8,1024]{2,0,1:T(4,128)(2,1)S(1)} %copy.27), channel_id=1, source_target_pairs={{0,128},{1,129},{2,130},{3,131},{4,132},{5,133},{6,134},{7,135},{8... | collective-permute-start | bytes 196616 | tf_op jit(solution)/shard_map/ppermute | solution.py:19
  57.5 108.0 %all-reduce.5.cloned.1.call-start = ((), (), s32[]{:S(2)}) async-start(), calls=%async_computation.2 | async-start | bytes 1048576 | tf_op jit(solution)/shard_map/psum | solution.py:114
  94.0 2.9 copy-start.6
  94.0 71.5 %copy-start.2 = (bf16[512,512]{1,0:T(8,128)(2,1)S(1)}, bf16[512,512]{1,0:T(8,128)(2,1)}, u32[]{:S(2)}) copy-start(bf16[512,512]{1,0:T(8,128)(2,1)} %param.16) | copy-start | bytes 1572868
  96.9 237.5 %all-reduce.9.cloned.1.call-start = ((), (), s32[]{:S(2)}) async-start(), calls=%async_computation.5 | async-start | bytes 7340032 | tf_op jit(solution)/shard_map/psum | solution.py:130
  198.6 3.7 copy-start.3
  198.6 3.7 copy-start.7
  204.7 204.3 %all-reduce.7.cloned.1.call-start = ((), (), s32[]{:S(2)}) async-start(), calls=%async_computation.3 | async-start | bytes 1048576 | tf_op jit(solution)/shard_map/psum | solution.py:134
  426.0 6.2 %collective-permute-start.1 = (bf16[4,4096]{1,0:T(4,128)(2,1)S(1)}, bf16[4,4096]{1,0:T(4,128)(2,1)S(1)}, u32[]{:S(2)}, u32[]{:S(2)}) collective-permute-start(bf16[4,4096]{1,0:T(4,128)(2,1)S(1)} %slice.46), channel_id=1, source_target_pairs={{128,0},{129,1},{130,2},{131,3},{132,4},{133,5},{134,6},{135,7},{1... | collective-permute-start | bytes 98312 | tf_op jit(solution)/shard_map/ppermute | solution.py:19
Sparse Core Ops, SparseCore 0:
  57.7 34.5 all-gather.2
  97.0 68.4 all-reduce.4
  204.8 129.5 all-reduce.8
  339.1 69.8 all-reduce.6
where the time goes:
time: 440 us; the launch traced here: 439 us
  waiting for transfers between devices  309 us (70%)
  blocking collectives  63.1 us (14%)
  local copies, waits for them, and re-layouts  19 us (4%)
  matrix products  15.5 us (4%)
  between operations  13.3 us (3%)
  other arithmetic  12.2 us (3%)
  starting transfers between devices  7.07 us (2%)
    psum x1, waiting for transfers between devices, local(): lax.psum(up_part.astype(jnp.bfloat16), 'col').astype(jnp.float32)  130 us
    psum x1, waiting for transfers between devices, local(): lax.psum(down_part.astype(jnp.bfloat16), 'row').astype(jnp.float32)  70 us
    psum x1, waiting for transfers between devices, local(): lax.psum(partial_value.reshape(total_rows, col_width).astype(jnp.bfloat16...  68.6 us
    all_gather x1, waiting for transfers between devices, local(): lax.all_gather(sectioned, 'col', axis=1, tiled=True)  34.6 us
    psum x1, blocking collectives, local(): squares = lax.psum(jnp.sum(stream * stream, axis=1), 'col')  31.7 us
    all_to_all x1, blocking collectives, local(): lax.all_to_all(mine_rows, 'col', split_axis=0, concat_axis=1, tiled=True)  16.1 us
    all_to_all x1, blocking collectives, local(): lax.all_to_all(moved, 'row', split_axis=1, concat_axis=0, tiled=True)  15.3 us
    unnamed x21, local copies, waits for them, and re-layouts  12.2 us
  transfers between devices with their start and end apart: 6, of which 6 were waited for; matrix products, arithmetic and copies ran while one was open for 0% of the time, Pallas kernels for 0%

commit v1 on v0

--- a/solution.py
+++ b/solution.py
@@ -111,8 +111,9 @@
     )
     col_width = out_block.shape[1]
     total_rows = row_count * col_count * slot_count
-    projected = lax.psum(
-        partial_value.reshape(total_rows, col_width).astype(jnp.bfloat16), "row"
+    projected = jnp.sum(
+        lax.all_gather(partial_value.reshape(total_rows, col_width).astype(jnp.bfloat16), "row"),
+        axis=0,
     ).astype(jnp.float32)
     stream = residual.astype(jnp.float32) + projected
     squares = lax.psum(jnp.sum(stream * stream, axis=1), "col")

time: 440 us -> 426 us (0.968)
  waiting for transfers between devices: 309 us -> 298 us
  blocking collectives: 63.1 us -> 58.6 us
    psum x1 -> x0, waiting for transfers between devices: 68.6 us -> none  [local(): lax.psum(partial_value.reshape(total_rows, col_width).astype(jnp.bfloat16...]
    all_gather x0 -> x1, waiting for transfers between devices: none -> 54.6 us  [local(): lax.all_gather(partial_value.reshape(total_rows, col_width).astype(jnp.bf...]
    psum x1, blocking collectives: 31.7 us -> 27.2 us  [local(): squares = lax.psum(jnp.sum(stream * stream, axis=1), 'col')]
where the time goes in v1:
time: 426 us
  waiting for transfers between devices  298 us (70%)
  blocking collectives  58.6 us (14%)
  local copies, waits for them, and re-layouts  19 us (4%)
  other arithmetic  15.3 us (4%)
  matrix products  14.2 us (3%)
  between operations  13.4 us (3%)
  starting transfers between devices  7.2 us (2%)
    psum x1, waiting for transfers between devices, local(): lax.psum(up_part.astype(jnp.bfloat16), 'col').astype(jnp.float32)  133 us
    psum x1, waiting for transfers between devices, local(): lax.psum(down_part.astype(jnp.bfloat16), 'row').astype(jnp.float32)  70 us
    all_gather x1, waiting for transfers between devices, local(): lax.all_gather(partial_value.reshape(total_rows, col_width).astype(jnp.bf...  54.6 us
    all_gather x1, waiting for transfers between devices, local(): lax.all_gather(sectioned, 'col', axis=1, tiled=True)  34.6 us
    psum x1, blocking collectives, local(): squares = lax.psum(jnp.sum(stream * stream, axis=1), 'col')  27.2 us
    all_to_all x1, blocking collectives, local(): lax.all_to_all(mine_rows, 'col', split_axis=0, concat_axis=1, tiled=True)  16.1 us
    all_to_all x1, blocking collectives, local(): lax.all_to_all(moved, 'row', split_axis=1, concat_axis=0, tiled=True)  15.3 us
    unnamed x21, local copies, waits for them, and re-layouts  12.2 us
  transfers between devices with their start and end apart: 6, of which 6 were waited for; matrix products, arithmetic and copies ran while one was open for 0% of the time, Pallas kernels for 0%

profile of v1, /device:TPU:1, one launch (start us, length us, event | category | flops | bytes accessed | tf_op | source)
XLA Modules:
  0.0 425.7 jit_solution(523211680710189439)
XLA Ops:
  6.5 0.8 convert_element_type.84
  7.3 0.7 multiply_add_fusion
  8.0 0.7 iota_compare_fusion
  8.7 3.9 copy.23
  12.7 4.2 fusion.50
  16.8 3.8 copy.32
  20.6 3.8 copy.33
  24.9 1.9 multiply_cosine_fusion
  27.1 4.7 %subtract_convert_fusion = (bf16[4,256,8,64]{3,1,2,0:T(8,128)(2,1)S(1)}, bf16[4,256,8,64]{3,1,2,0:T(8,128)(2,1)S(1)}) fusion(f32[4,256,8,64]{3,1,2,0:T(8,128)} %copy.33, f32[4,256,8,64]{3,1,2,0:T(8,128)} %copy.32, f32[4,256,64]{2,1,0:T(8,128)S(1)} %get-tuple-element.22, f32[4,256,64]{2,1,0:T(8,128)S(1)} %get-tuple-element.21), kind=kLoop, calls=%fused_computation.3 | loop fusion | flops 4194304 | bytes 6815744 | tf_op jit(solution)/shard_map/convert.7
  31.8 1.3 select_reduce_fusion
  33.4 0.6 copy.36
  34.6 5.8 %collective-permute-start = (bf16[4,8,1024]{2,0,1:T(4,128)(2,1)S(1)}, bf16[4,8,1024]{2,0,1:T(4,128)(2,1)S(1)}, u32[]{:S(2)}, u32[]{:S(2)}) collective-permute-start(bf16[4,8,1024]{2,0,1:T(4,128)(2,1)S(1)} %copy.27), channel_id=1, source_target_pairs={{0,128},{1,129},{2,130},{3,131},{4,132},{5,133},{6,134},{7,135},{8... | collective-permute-start | bytes 196616 | tf_op jit(solution)/shard_map/ppermute | solution.py:19
  40.4 1.3 collective-permute-done
  41.7 15.3 %all_to_all.34 = bf16[4,8,1024]{2,0,1:T(4,128)(2,1)S(1)} all-to-all(bf16[4,8,1024]{2,0,1:T(4,128)(2,1)S(1)} %collective-permute-done), channel_id=1, replica_groups=mesh['side'=2,'row'=8,'col'=16] {'row'}, dimensions={1} | all-to-all | bytes 131072 | tf_op jit(solution)/shard_map/all_to_all | solution.py:103
  57.0 0.6 copy.28
  57.7 34.6 %all-gather.5.cloned.1.call-done = bf16[8,64,1,1024]{3,0,2,1:T(8,128)(2,1)} async-done(((bf16[8,4,1,1024]{3,0,2,1:T(8,128)(2,1)}), bf16[8,64,1,1024]{3,0,2,1:T(8,128)(2,1)}) %all-gather.5.cloned.1.call-update) | async-done | bytes 1048592 | tf_op jit(solution)/shard_map/all_gather | solution.py:108
  92.4 1.8 copy.29
  94.2 1.5 convolution_convert_fusion.2
  95.8 54.6 %all-gather.7.cloned.1.call-done = bf16[4096,512]{1,0:T(8,128)(2,1)} async-done(((bf16[512,512]{1,0:T(8,128)(2,1)}), bf16[4096,512]{1,0:T(8,128)(2,1)}) %all-gather.7.cloned.1.call-update) | async-done | bytes 4194320 | tf_op jit(solution)/shard_map/all_gather | solution.py:115
  150.4 3.1 reduce_sum.31
  153.5 1.3 multiply_reduce_fusion
  154.7 27.2 %psum.28 = f32[512]{0:T(512)S(1)} all-reduce(f32[512]{0:T(512)S(1)} %get-tuple-element.13), channel_id=1, replica_groups=mesh['side'=2,'row'=8,'col'=16] {'col'}, use_global_device_ids=true, to_apply=%region_4.5 | all-reduce | flops 512 | bytes 4096 | tf_op jit(solution)/shard_map/psum | solution.py:119
  181.9 3.6 convolution_convert_fusion.1
  185.6 2.5 convolution_convert_fusion
  188.1 132.6 %all-reduce.6.cloned.1.call-done = (bf16[512,1792]{1,0:T(8,128)(2,1)}, bf16[512,1792]{1,0:T(8,128)(2,1)}) async-done(((bf16[512,1792]{1,0:T(8,128)(2,1)}, bf16[512,1792]{1,0:T(8,128)(2,1)}), (bf16[512,1792]{1,0:T(8,128)(2,1)}, bf16[512,1792]{1,0:T(8,128)(2,1)})) %all-reduce.6.cloned.1.call-update) | async-done | bytes 3670032 | tf_op jit(solution)/shard_map/psum | solution.py:131
  320.7 4.6 %fusion.16 = bf16[512,512]{1,0:T(8,128)(2,1)} fusion(bf16[1,1792,512]{2,1,0:T(8,128)(2,1)} %param.21, bf16[512,1792]{1,0:T(8,128)(2,1)} %get-tuple-element.5, bf16[512,1792]{1,0:T(8,128)(2,1)} %get-tuple-element.6), kind=kOutput, calls=%fused_computation.21 | convolution fusion | flops 947126272 | bytes 6029312 | tf_op jit(solution)/shard_map/dot_general | solution.py:134
  325.4 70.0 %all-reduce.4.cloned.1.call-done = bf16[512,512]{1,0:T(8,128)(2,1)} async-done(((bf16[512,512]{1,0:T(8,128)(2,1)}), bf16[512,512]{1,0:T(8,128)(2,1)}) %all-reduce.4.cloned.1.call-update) | async-done | bytes 524304 | tf_op jit(solution)/shard_map/psum | solution.py:135
  395.4 0.9 fusion.37
  396.3 16.1 %all_to_all.35 = bf16[16,4,512]{2,1,0:T(4,128)(2,1)S(1)} all-to-all(bf16[16,4,512]{2,1,0:T(4,128)(2,1)S(1)} %all_to_all.28), channel_id=1, replica_groups=mesh['side'=2,'row'=8,'col'=16] {'col'}, dimensions={0} | all-to-all | bytes 131072 | tf_op jit(solution)/shard_map/all_to_all | solution.py:139
  412.3 1.3 collective-permute-start.1
  413.6 4.9 %collective-permute-done.1 = bf16[4,4096]{1,0:T(4,128)(2,1)S(1)} collective-permute-done((bf16[4,4096]{1,0:T(4,128)(2,1)S(1)}, bf16[4,4096]{1,0:T(4,128)(2,1)S(1)}, u32[]{:S(2)}, u32[]{:S(2)}) %collective-permute-start.1) | collective-permute-done | bytes 32800 | tf_op jit(solution)/shard_map/ppermute | solution.py:19
  418.5 0.6 slice_select_fusion
  (45 shorter events, 1.7 us)
Async XLA Ops:
  6.5 175.4 %copy-start = (bf16[1,512,1792]{2,1,0:T(8,128)(2,1)S(1)}, bf16[1,512,1792]{2,1,0:T(8,128)(2,1)}, u32[]{:S(2)}) copy-start(bf16[1,512,1792]{2,1,0:T(8,128)(2,1)} %param.19) | copy-start | bytes 5505028
  6.5 85.8 %all-gather.5.cloned.1.call-start = ((), (), s32[]{:S(2)}) async-start(), calls=%async_computation.3 | async-start | bytes 1114112 | tf_op jit(solution)/shard_map/all_gather | solution.py:108
  20.6 3.8 copy-start.3
  20.6 3.9 copy-start.4
  31.8 1.6 copy-start.1
  34.5 59.7 %copy-start.7 = (bf16[1,1024,512]{2,1,0:T(8,128)(2,1)S(1)}, bf16[1,1024,512]{2,1,0:T(8,128)(2,1)}, u32[]{:S(2)}) copy-start(bf16[1,1024,512]{2,1,0:T(8,128)(2,1)} %param.18) | copy-start | bytes 3145732
  34.6 7.1 %collective-permute-start = (bf16[4,8,1024]{2,0,1:T(4,128)(2,1)S(1)}, bf16[4,8,1024]{2,0,1:T(4,128)(2,1)S(1)}, u32[]{:S(2)}, u32[]{:S(2)}) collective-permute-start(bf16[4,8,1024]{2,0,1:T(4,128)(2,1)S(1)} %copy.27), channel_id=1, source_target_pairs={{0,128},{1,129},{2,130},{3,131},{4,132},{5,133},{6,134},{7,135},{8... | collective-permute-start | bytes 196616 | tf_op jit(solution)/shard_map/ppermute | solution.py:19
  57.7 92.7 %all-gather.7.cloned.1.call-start = ((), (), s32[]{:S(2)}) async-start(), calls=%async_computation.4 | async-start | bytes 4718592 | tf_op jit(solution)/shard_map/all_gather | solution.py:115
  94.2 1.6 copy-start.5
  95.7 225.0 %all-reduce.6.cloned.1.call-start = ((), (), s32[]{:S(2)}) async-start(), calls=%async_computation.5 | async-start | bytes 7340032 | tf_op jit(solution)/shard_map/psum | solution.py:131
  181.9 3.7 copy-start.2
  181.9 3.7 copy-start.6
  188.1 207.3 %all-reduce.4.cloned.1.call-start = ((), (), s32[]{:S(2)}) async-start(), calls=%async_computation.2 | async-start | bytes 1048576 | tf_op jit(solution)/shard_map/psum | solution.py:135
  412.3 6.2 %collective-permute-start.1 = (bf16[4,4096]{1,0:T(4,128)(2,1)S(1)}, bf16[4,4096]{1,0:T(4,128)(2,1)S(1)}, u32[]{:S(2)}, u32[]{:S(2)}) collective-permute-start(bf16[4,4096]{1,0:T(4,128)(2,1)S(1)} %slice.46), channel_id=1, source_target_pairs={{128,0},{129,1},{130,2},{131,3},{132,4},{133,5},{134,6},{135,7},{1... | collective-permute-start | bytes 98312 | tf_op jit(solution)/shard_map/ppermute | solution.py:19
Sparse Core Ops, SparseCore 0:
  57.8 34.5 all-gather.4
  95.8 54.5 all-gather.6
  188.2 132.4 all-reduce.5
  325.5 69.8 all-reduce.3
